TPU v7x, 32 devices: a whole 2x2x4 slice. The times are simulated.
32 devices in a mesh: lon: 4 (over y, x), lat: 8 (over z, core).
Axes of the slice: x: 2, y: 2, z: 4, core: 2. Of those that a mesh axis runs over, the one named last changes fastest.
Arguments:
- state_adjoint: float32 [4, 4, 512, 1024], P(None, None, 'lat', 'lon'), may hold values from -6 to 6
- east_velocity: float32 [4, 512, 1024], P(None, 'lat', 'lon'), may hold values from -1.2 to 1.2
- north_velocity: float32 [4, 512, 1024], P(None, 'lat', 'lon'), may hold values from -1.2 to 1.2
- ocean_mask: int32 [4, 512, 1024], P(None, 'lat', 'lon'), may hold values 0 or 1
- partner: int32 [1024], P('lon'), may hold values from 0 to 1023, as said below
Outputs:
- sensitivity: float32 [4, 4, 512, 1024], P(None, None, 'lat', 'lon')
Inputs may be any that keep to these rules, and one draw needn't show every extreme that they name: partner[i] = (c - i) mod 1024 with one c for all columns, 1023 <= c <= 1278; hence partner[partner[i]] = i.
All inputs are finite; a program needn't handle non-finite values. No bound on the sum of `ocean_mask` on one device may be relied on, other than what follows from the above.
Results may differ from a plain program's by a relative error of at most 0.00002.
Values sent between devices are 32-bit elements; how exact they have to be, the bound alone decides.
No kernel may reach another device: no remote copies, remote signals or barrier semaphores. Data moves between devices by JAX's collectives and lax.ppermute only.
A program may use at most 64 MiB of HBM per device.

v0:
```python
import jax
import jax.numpy as jnp
from jax import lax
from jax.sharding import PartitionSpec as P

STEPS = 2


def shifted(shard, axis, by):
    count = lax.axis_size(axis)
    return lax.ppermute(shard, axis, [(i, (i + by) % count) for i in range(count)])


def shifted_2(shard, axis, by):
    count = lax.axis_size(axis)
    pairs = [(i, i + by) for i in range(count) if 0 <= i + by < count]
    return lax.ppermute(shard, axis, pairs)


def with_halo(block, sides, width, periodic):
    for axis, dim in sides:
        count = lax.axis_size(axis)
        forward = [(i, i + 1) for i in range(count - 1)]
        if periodic:
            forward.append((count - 1, 0))
        backward = [(target, source) for source, target in forward]
        low = lax.ppermute(
            lax.slice_in_dim(block, block.shape[dim] - width, None, axis=dim), axis, forward
        )
        high = lax.ppermute(lax.slice_in_dim(block, 0, width, axis=dim), axis, backward)
        block = jnp.concatenate([low, block, high], axis=dim)
    return block


def per_device(state_adjoint, east_velocity, north_velocity, ocean_mask, partner):
    wet_cells = ocean_mask.astype(jnp.float32)
    fold_signs = jnp.array([1.0, 1.0, -1.0, -1.0], dtype=jnp.float32).reshape(4, 1, 1)
    lat_place = lax.axis_index("lat")
    lat_count = lax.axis_size("lat")
    is_top = (lat_place == lat_count - 1).astype(jnp.float32)
    speed_west_edge = shifted(east_velocity[:, :, -1:], "lon", 1)
    speed_south_edge = shifted_2(north_velocity[:, -1:, :], "lat", 1)
    west_speed = jnp.concatenate([speed_west_edge, east_velocity[:, :, :-1]], axis=2)
    south_speed = jnp.concatenate([speed_south_edge, north_velocity[:, :-1, :]], axis=1)
    fold_weight = 1.0 + north_velocity[:, -1, :]
    current = state_adjoint
    for iteration in range(STEPS):
        masked = wet_cells * current
        lon_padded = with_halo(masked, (("lon", 3),), 1, True)
        lat_padded = with_halo(masked, (("lat", 2),), 1, False)
        west_rim = lon_padded[:, :, :, 0]
        east_rim = lon_padded[:, :, :, -1]
        south_rim = lat_padded[:, :, 0, :]
        north_rim = lat_padded[:, :, -1, :]
        east_adj = jnp.concatenate([masked[..., 1:], east_rim[..., None]], axis=3)
        west_adj = jnp.concatenate([west_rim[..., None], masked[..., :-1]], axis=3)
        north_adj = jnp.concatenate([masked[:, :, 1:, :], north_rim[:, :, None, :]], axis=2)
        south_adj = jnp.concatenate([south_rim[:, :, None, :], masked[:, :, :-1, :]], axis=2)
        transport = (
            0.5 * east_velocity * (east_adj - masked)
            + 0.5 * west_speed * (masked - west_adj)
            + 0.5 * north_velocity * (north_adj - masked)
            + 0.5 * south_speed * (masked - south_adj)
        )
        fold_flux = fold_weight * masked[:, :, -1, :]
        whole_row = lax.all_gather(fold_flux, "lon", axis=2, tiled=True)
        picked = jnp.take(whole_row, partner, axis=2)
        folded = 0.5 * fold_signs * picked
        total = masked + transport
        total = total.at[:, :, -1, :].add(is_top * folded)
        current = wet_cells * total
    return current


def solution(mesh):
    placed = (
        P(None, None, "lat", "lon"),
        P(None, "lat", "lon"),
        P(None, "lat", "lon"),
        P(None, "lat", "lon"),
        P("lon"),
    )
    return jax.shard_map(
        per_device,
        mesh=mesh,
        in_specs=placed,
        out_specs=P(None, None, "lat", "lon"),
        check_vma=False,
    )
```

profile of v0, /device:TPU:10, one launch (start us, length us, event | category | flops | bytes accessed | tf_op | source)
XLA Modules:
  0.0 109.1 jit_solution(16763126374377405692)
XLA Ops:
  0.0 0.8 broadcast_add_fusion
  0.8 1.9 %collective-permute-start.4 = (f32[4,1,256]{2,1,0:T(1,128)S(1)}, f32[4,1,256]{2,1,0:T(1,128)S(1)}, u32[]{:S(2)}, u32[]{:S(2)}) collective-permute-start(f32[4,1,256]{2,1,0:T(1,128)S(1)} %get-tuple-element.47), channel_id=1, source_target_pairs={{0,1},{1,2},{2,3},{3,4},{4,5},{5,6},{6,7},{8,9},{9,10},{10,11},{11... | collective-permute-start | bytes 12296 | tf_op jit(solution)/shard_map/ppermute | solution.py:17
  2.7 1.7 %slice.119 = f32[4,64,1]{2,1,0:T(8,128)} slice(f32[4,64,256]{2,1,0:T(8,128)} %param.13), slice={[0:4], [0:64], [255:256]} | slice | bytes 2048 | tf_op jit(solution)/shard_map/slice | solution.py:41
  4.3 1.5 %collective-permute-start.1 = (f32[4,64,1]{2,1,0:T(8,128)}, f32[4,64,1]{2,1,0:T(8,128)}, u32[]{:S(2)}, u32[]{:S(2)}) collective-permute-start(f32[4,64,1]{2,1,0:T(8,128)} %slice.119), channel_id=1, source_target_pairs={{0,8},{8,16},{16,24},{24,0},{1,9},{9,17},{17,25},{25,1},{2,10},{10... | collective-permute-start | bytes 3080 | tf_op jit(solution)/shard_map/ppermute | solution.py:11
  5.8 1.0 convert_element_type.6
  6.8 0.2 copy.78
  7.0 0.0 copy-start.8
  7.0 0.0 copy-start.4
  7.0 0.0 copy-start.5
  7.0 2.1 %copy_multiply_fusion = f32[4,4,64,256]{3,1,0,2:T(4,128)S(1)} fusion(f32[4,4,64,256]{3,2,1,0:T(8,128)} %param.12, f32[4,64,256]{2,0,1:T(4,128)S(1)} %copy.78), kind=kLoop, calls=%fused_computation.26 | loop fusion | flops 262144 | bytes 2359296 | tf_op jit(solution)/shard_map/mul | solution.py:48
  9.1 3.3 %collective-permute-start.5 = (f32[4,4,1,256]{3,1,0,2:T(4,128)S(1)}, f32[4,4,1,256]{3,1,0,2:T(4,128)S(1)}, u32[]{:S(2)}, u32[]{:S(2)}) collective-permute-start(f32[4,4,1,256]{3,1,0,2:T(4,128)S(1)} %get-tuple-element.38), channel_id=1, source_target_pairs={{0,1},{1,2},{2,3},{3,4},{4,5},{5,6},{6,7},{8,9},{9,10},{10,11},{11... | collective-permute-start | bytes 49160 | tf_op jit(solution)/shard_map/ppermute | solution.py:27
  12.4 2.3 %collective-permute-start.3 = (f32[4,4,1,256]{3,1,0,2:T(4,128)S(1)}, f32[4,4,1,256]{3,1,0,2:T(4,128)S(1)}, u32[]{:S(2)}, u32[]{:S(2)}) collective-permute-start(f32[4,4,1,256]{3,1,0,2:T(4,128)S(1)} %get-tuple-element.39), channel_id=1, source_target_pairs={{1,0},{2,1},{3,2},{4,3},{5,4},{6,5},{7,6},{9,8},{10,9},{11,10},{12... | collective-permute-start | bytes 49160 | tf_op jit(solution)/shard_map/ppermute | solution.py:30
  14.7 1.3 %fusion.26 = (f32[4,4,64,1]{3,1,0,2:T(4,128)}, f32[4,4,64,1]{3,1,0,2:T(4,128)}) fusion(f32[4,4,64,256]{3,1,0,2:T(4,128)S(1)} %copy_multiply_fusion), kind=kLoop, calls=%fused_computation.54 | loop fusion | bytes 16384 | tf_op jit(solution)/shard_map/slice | solution.py:28
  16.0 1.5 %collective-permute-start.2 = (f32[4,4,64,1]{3,1,0,2:T(4,128)}, f32[4,4,64,1]{3,1,0,2:T(4,128)}, u32[]{:S(2)}, u32[]{:S(2)}) collective-permute-start(f32[4,4,64,1]{3,1,0,2:T(4,128)} %get-tuple-element.42), channel_id=1, source_target_pairs={{0,8},{8,16},{16,24},{24,0},{1,9},{9,17},{17,25},{25,1},{2,10},{10... | collective-permute-start | bytes 12296 | tf_op jit(solution)/shard_map/ppermute | solution.py:27
  17.5 0.0 copy-done.8
  17.5 0.5 compare_and_fusion
  18.0 0.0 copy-done.4
  18.0 0.0 copy-done.5
  18.1 1.8 %fusion.25 = (f32[4,4,63,256]{3,1,0,2:T(4,128)}, f32[4,4,63,256]{3,1,0,2:T(4,128)}) fusion(f32[4,4,64,256]{3,1,0,2:T(4,128)S(1)} %copy_multiply_fusion), kind=kLoop, calls=%fused_computation.53 | loop fusion | bytes 4128768 | tf_op jit(solution)/shard_map/slice | solution.py:58
  19.9 1.7 %fusion.27 = (f32[4,4,64,255]{3,1,0,2:T(4,128)S(1)}, f32[4,4,64,255]{3,1,0,2:T(4,128)}) fusion(f32[4,4,64,256]{3,1,0,2:T(4,128)S(1)} %copy_multiply_fusion), kind=kLoop, calls=%fused_computation.55 | loop fusion | bytes 4177920 | tf_op jit(solution)/shard_map/slice | solution.py:56
  21.6 12.3 %all_gather.6 = f32[4,4,1024]{2,1,0:T(4,128)S(1)} all-gather(f32[4,4,256]{2,1,0:T(4,128)S(1)} %bitcast_multiply_fusion.3), channel_id=1, replica_groups=mesh['lon'=4,'lat'=8] {'lon'}, dimensions={2}, use_global_device_ids=true | all-gather | bytes 81920 | tf_op jit(solution)/shard_map/all_gather | solution.py:66
  33.9 0.9 copy.80
  34.8 0.9 copy.82
  35.7 1.7 %copy.84 = f32[4,4,1024]{1,0,2:T(4,128)} copy(f32[4,4,1024]{2,1,0:T(4,128)S(1)} %all_gather.6) | data formatting | bytes 131072 | tf_op jit(solution)/shard_map/all_gather | solution.py:66
  37.4 2.6 %gather_fusion = f32[256,4,4]{2,1,0:T(4,128)S(1)} fusion(f32[4,4,1024]{1,0,2:T(4,128)} %copy.84, s32[1024]{0:T(1024)S(1)} %pad_clamp_fusion), kind=kCustom, calls=%fused_computation.clone | custom fusion | bytes 33792 | tf_op jit(solution)/shard_map/jit(_take)/gather | solution.py:67
  40.0 0.2 copy.85
  40.2 0.0 collective-permute-done.1
  40.2 0.4 collective-permute-start
  40.6 1.0 maximum_multiply_fusion
  41.6 0.2 copy.81
  41.8 0.0 copy-start.2
  41.8 0.0 collective-permute-done.4
  41.9 0.2 copy.83
  42.1 0.0 copy-start.3
  42.1 0.0 collective-permute-done.2
  42.1 12.2 %collective-permute-done = f32[4,4,64,1]{3,1,0,2:T(4,128)S(1)} collective-permute-done((f32[4,4,64,1]{3,1,0,2:T(4,128)}, f32[4,4,64,1]{3,1,0,2:T(4,128)S(1)}, u32[]{:S(2)}, u32[]{:S(2)}) %collective-permute-start) | collective-permute-done | bytes 4128 | tf_op jit(solution)/shard_map/ppermute | solution.py:30
  54.3 0.0 collective-permute-done.5
  54.3 0.0 collective-permute-done.3
  54.3 0.0 copy-done
  54.3 0.0 copy-done.1
  54.3 0.0 copy-start.6
  54.4 0.0 copy-start.7
  54.4 4.6 %fusion.4 = f32[4,4,64,256]{3,1,0,2:T(4,128)S(1)} fusion(f32[4,4,64,1]{3,1,0,2:T(4,128)S(1)} %collective-permute-done, f32[4,4,64,255]{3,1,0,2:T(4,128)} %get-tuple-element.45, f32[4,4,64,255]{3,1,0,2:T(4,128)S(1)} %get-tuple-element.44, f32[4,4,64,1]{3,1,0,2:T(4,128)} %collective-permute-done.2, f32[4,4,1,256]{3,1,0,2:T(4,128)S(1)} %collective-permute-done.3, ...), kind=kLoop, calls=%fused_computation.7 | loop fusion | flops 4456448 | bytes 7602176 | tf_op jit(solution)/shard_map/add | solution.py:69
  59.0 0.1 fusion.17
  59.1 0.3 multiply_multiply_fusion
  59.5 1.4 %fusion.22 = (f32[4,4,64,1]{3,1,0,2:T(4,128)}, f32[4,4,64,1]{3,1,0,2:T(4,128)}) fusion(f32[4,4,64,256]{3,1,0,2:T(4,128)S(1)} %multiply_multiply_fusion), kind=kLoop, calls=%fused_computation.50 | loop fusion | bytes 16384 | tf_op jit(solution)/shard_map/slice | solution.py:28
  60.8 1.8 %fusion.21 = (f32[4,4,63,256]{3,1,0,2:T(4,128)}, f32[4,4,63,256]{3,1,0,2:T(4,128)}) fusion(f32[4,4,64,256]{3,1,0,2:T(4,128)S(1)} %multiply_multiply_fusion), kind=kLoop, calls=%fused_computation.49 | loop fusion | bytes 4128768 | tf_op jit(solution)/shard_map/slice | solution.py:58
  62.6 0.7 fusion.23
  63.4 1.9 %collective-permute-start.9 = (f32[4,4,1,256]{3,1,0,2:T(4,128)S(1)}, f32[4,4,1,256]{3,1,0,2:T(4,128)S(1)}, u32[]{:S(2)}, u32[]{:S(2)}) collective-permute-start(f32[4,4,1,256]{3,1,0,2:T(4,128)S(1)} %get-tuple-element.30), channel_id=1, source_target_pairs={{0,1},{1,2},{2,3},{3,4},{4,5},{5,6},{6,7},{8,9},{9,10},{10,11},{11... | collective-permute-start | bytes 49160 | tf_op jit(solution)/shard_map/ppermute | solution.py:27
  65.3 3.6 %collective-permute-start.8 = (f32[4,4,1,256]{3,1,0,2:T(4,128)S(1)}, f32[4,4,1,256]{3,1,0,2:T(4,128)S(1)}, u32[]{:S(2)}, u32[]{:S(2)}) collective-permute-start(f32[4,4,1,256]{3,1,0,2:T(4,128)S(1)} %get-tuple-element.31), channel_id=1, source_target_pairs={{1,0},{2,1},{3,2},{4,3},{5,4},{6,5},{7,6},{9,8},{10,9},{11,10},{12... | collective-permute-start | bytes 49160 | tf_op jit(solution)/shard_map/ppermute | solution.py:30
  69.0 0.4 collective-permute-start.7
  69.4 1.7 %collective-permute-start.6 = (f32[4,4,64,1]{3,1,0,2:T(4,128)}, f32[4,4,64,1]{3,1,0,2:T(4,128)}, u32[]{:S(2)}, u32[]{:S(2)}) collective-permute-start(f32[4,4,64,1]{3,1,0,2:T(4,128)} %get-tuple-element.35), channel_id=1, source_target_pairs={{8,0},{16,8},{24,16},{0,24},{9,1},{17,9},{25,17},{1,25},{10,2},{18... | collective-permute-start | bytes 12296 | tf_op jit(solution)/shard_map/ppermute | solution.py:30
  71.0 25.6 %all_gather.7 = f32[4,4,1024]{2,1,0:T(4,128)S(1)} all-gather(f32[4,4,256]{2,1,0:T(4,128)S(1)} %bitcast_multiply_fusion.1), channel_id=1, replica_groups=mesh['lon'=4,'lat'=8] {'lon'}, dimensions={2}, use_global_device_ids=true | all-gather | bytes 81920 | tf_op jit(solution)/shard_map/all_gather | solution.py:66
  96.7 1.7 %copy.86 = f32[4,4,1024]{1,0,2:T(4,128)} copy(f32[4,4,1024]{2,1,0:T(4,128)S(1)} %all_gather.7) | data formatting | bytes 131072 | tf_op jit(solution)/shard_map/all_gather | solution.py:66
  98.4 3.4 %gather_fusion.1 = f32[256,4,4]{2,1,0:T(4,128)} fusion(f32[4,4,1024]{1,0,2:T(4,128)} %copy.86, s32[1024]{0:T(1024)S(1)} %pad_clamp_fusion), kind=kCustom, calls=%fused_computation.1.clone | custom fusion | bytes 33792 | tf_op jit(solution)/shard_map/jit(_take)/gather | solution.py:67
  101.7 1.2 %copy.87 = f32[256,4,4]{0,2,1:T(4,128)S(1)} copy(f32[256,4,4]{2,1,0:T(4,128)} %gather_fusion.1) | data formatting | bytes 32768 | tf_op jit(solution)/shard_map/jit(_take)/gather | solution.py:67
  103.0 0.0 collective-permute-done.7
  103.0 0.0 collective-permute-done.6
  103.0 0.0 collective-permute-done.9
  103.0 0.0 collective-permute-done.8
  103.0 4.1 %fusion.12 = f32[4,4,64,256]{3,1,0,2:T(4,128)S(1)} fusion(f32[4,4,64,1]{3,1,0,2:T(4,128)} %collective-permute-done.6, f32[4,4,64,255]{3,1,0,2:T(4,128)S(1)} %get-tuple-element.37, f32[4,4,64,255]{3,1,0,2:T(4,128)S(1)} %get-tuple-element.36, f32[4,4,64,1]{3,1,0,2:T(4,128)} %collective-permute-done.7, f32[4,4,1,256]{3,1,0,2:T(4,128)S(1)} %collective-permute-done.8, ...), kind=kLoop, calls=%fused_computation.19 | loop fusion | flops 4718592 | bytes 7602176 | tf_op jit(solution)/shard_map/add | solution.py:69
  107.1 0.1 fusion.16
  107.2 0.3 broadcast_multiply_fusion
  107.5 1.6 %copy.88 = f32[4,4,64,256]{3,2,1,0:T(8,128)} copy(f32[4,4,64,256]{3,1,0,2:T(4,128)S(1)} %broadcast_multiply_fusion) | data formatting | bytes 2097152 | tf_op jit(solution)/shard_map/mul | solution.py:71
  (16 shorter events, 0.1 us)
Async XLA Ops:
  0.8 41.1 %collective-permute-start.4 = (f32[4,1,256]{2,1,0:T(1,128)S(1)}, f32[4,1,256]{2,1,0:T(1,128)S(1)}, u32[]{:S(2)}, u32[]{:S(2)}) collective-permute-start(f32[4,1,256]{2,1,0:T(1,128)S(1)} %get-tuple-element.47), channel_id=1, source_target_pairs={{0,1},{1,2},{2,3},{3,4},{4,5},{5,6},{6,7},{8,9},{9,10},{10,11},{11... | collective-permute-start | bytes 12296 | tf_op jit(solution)/shard_map/ppermute | solution.py:17
  4.3 35.8 %collective-permute-start.1 = (f32[4,64,1]{2,1,0:T(8,128)}, f32[4,64,1]{2,1,0:T(8,128)}, u32[]{:S(2)}, u32[]{:S(2)}) collective-permute-start(f32[4,64,1]{2,1,0:T(8,128)} %slice.119), channel_id=1, source_target_pairs={{0,8},{8,16},{16,24},{24,0},{1,9},{9,17},{17,25},{25,1},{2,10},{10... | collective-permute-start | bytes 3080 | tf_op jit(solution)/shard_map/ppermute | solution.py:11
  7.0 10.5 %copy-start.8 = (s32[256]{0:T(256)S(1)}, s32[256]{0:T(256)}, u32[]{:S(2)}) copy-start(s32[256]{0:T(256)} %param.16) | copy-start | bytes 3076
  7.0 11.0 %copy-start.4 = (f32[4,64,256]{2,1,0:T(8,128)S(1)}, f32[4,64,256]{2,1,0:T(8,128)}, u32[]{:S(2)}) copy-start(f32[4,64,256]{2,1,0:T(8,128)} %param.13) | copy-start | bytes 786436
  7.0 11.0 %copy-start.5 = (f32[4,64,256]{2,1,0:T(8,128)S(1)}, f32[4,64,256]{2,1,0:T(8,128)}, u32[]{:S(2)}) copy-start(f32[4,64,256]{2,1,0:T(8,128)} %param.14) | copy-start | bytes 786436
  9.1 45.2 %collective-permute-start.5 = (f32[4,4,1,256]{3,1,0,2:T(4,128)S(1)}, f32[4,4,1,256]{3,1,0,2:T(4,128)S(1)}, u32[]{:S(2)}, u32[]{:S(2)}) collective-permute-start(f32[4,4,1,256]{3,1,0,2:T(4,128)S(1)} %get-tuple-element.38), channel_id=1, source_target_pairs={{0,1},{1,2},{2,3},{3,4},{4,5},{5,6},{6,7},{8,9},{9,10},{10,11},{11... | collective-permute-start | bytes 49160 | tf_op jit(solution)/shard_map/ppermute | solution.py:27
  12.4 41.9 %collective-permute-start.3 = (f32[4,4,1,256]{3,1,0,2:T(4,128)S(1)}, f32[4,4,1,256]{3,1,0,2:T(4,128)S(1)}, u32[]{:S(2)}, u32[]{:S(2)}) collective-permute-start(f32[4,4,1,256]{3,1,0,2:T(4,128)S(1)} %get-tuple-element.39), channel_id=1, source_target_pairs={{1,0},{2,1},{3,2},{4,3},{5,4},{6,5},{7,6},{9,8},{10,9},{11,10},{12... | collective-permute-start | bytes 49160 | tf_op jit(solution)/shard_map/ppermute | solution.py:30
  16.0 26.0 %collective-permute-start.2 = (f32[4,4,64,1]{3,1,0,2:T(4,128)}, f32[4,4,64,1]{3,1,0,2:T(4,128)}, u32[]{:S(2)}, u32[]{:S(2)}) collective-permute-start(f32[4,4,64,1]{3,1,0,2:T(4,128)} %get-tuple-element.42), channel_id=1, source_target_pairs={{0,8},{8,16},{16,24},{24,0},{1,9},{9,17},{17,25},{25,1},{2,10},{10... | collective-permute-start | bytes 12296 | tf_op jit(solution)/shard_map/ppermute | solution.py:27
  35.7 18.7 %copy-start = (f32[4,4,64,256]{3,2,1,0:T(8,128)S(1)}, f32[4,4,64,256]{3,2,1,0:T(8,128)}, u32[]{:S(2)}) copy-start(f32[4,4,64,256]{3,2,1,0:T(8,128)} %param.12) | copy-start | bytes 3145732
  40.2 14.2 %copy-start.1 = (f32[4,64,256]{2,0,1:T(4,128)S(1)}, f32[4,64,256]{2,0,1:T(4,128)}, u32[]{:S(2)}) copy-start(f32[4,64,256]{2,0,1:T(4,128)} %copy.82) | copy-start | bytes 786436
  40.2 14.1 %collective-permute-start = (f32[4,4,64,1]{3,1,0,2:T(4,128)}, f32[4,4,64,1]{3,1,0,2:T(4,128)S(1)}, u32[]{:S(2)}, u32[]{:S(2)}) collective-permute-start(f32[4,4,64,1]{3,1,0,2:T(4,128)} %get-tuple-element.43), channel_id=1, source_target_pairs={{8,0},{16,8},{24,16},{0,24},{9,1},{17,9},{25,17},{1,25},{10,2},{18... | collective-permute-start | bytes 12296 | tf_op jit(solution)/shard_map/ppermute | solution.py:30
  41.8 17.2 %copy-start.2 = (f32[4,64,256]{2,0,1:T(4,128)}, f32[4,64,256]{2,0,1:T(4,128)S(1)}, u32[]{:S(2)}) copy-start(f32[4,64,256]{2,0,1:T(4,128)S(1)} %copy.81) | copy-start | bytes 786436
  42.1 17.0 %copy-start.3 = (f32[4,64,256]{2,0,1:T(4,128)}, f32[4,64,256]{2,0,1:T(4,128)S(1)}, u32[]{:S(2)}) copy-start(f32[4,64,256]{2,0,1:T(4,128)S(1)} %copy.83) | copy-start | bytes 786436
  54.3 4.7 %copy-start.6 = (f32[4]{0:T(128)S(1)}, f32[4]{0:T(128)}, u32[]{:S(2)}) copy-start(f32[4]{0:T(128)} %constant.73) | copy-start | bytes 52
  54.4 4.7 %copy-start.7 = (pred[256]{0:T(512)(128)(4,1)S(1)}, pred[256]{0:T(512)(128)(4,1)}, u32[]{:S(2)}) copy-start(pred[256]{0:T(512)(128)(4,1)} %compare_and_fusion) | copy-start | bytes 772
  63.4 39.6 %collective-permute-start.9 = (f32[4,4,1,256]{3,1,0,2:T(4,128)S(1)}, f32[4,4,1,256]{3,1,0,2:T(4,128)S(1)}, u32[]{:S(2)}, u32[]{:S(2)}) collective-permute-start(f32[4,4,1,256]{3,1,0,2:T(4,128)S(1)} %get-tuple-element.30), channel_id=1, source_target_pairs={{0,1},{1,2},{2,3},{3,4},{4,5},{5,6},{6,7},{8,9},{9,10},{10,11},{11... | collective-permute-start | bytes 49160 | tf_op jit(solution)/shard_map/ppermute | solution.py:27
  65.3 37.7 %collective-permute-start.8 = (f32[4,4,1,256]{3,1,0,2:T(4,128)S(1)}, f32[4,4,1,256]{3,1,0,2:T(4,128)S(1)}, u32[]{:S(2)}, u32[]{:S(2)}) collective-permute-start(f32[4,4,1,256]{3,1,0,2:T(4,128)S(1)} %get-tuple-element.31), channel_id=1, source_target_pairs={{1,0},{2,1},{3,2},{4,3},{5,4},{6,5},{7,6},{9,8},{10,9},{11,10},{12... | collective-permute-start | bytes 49160 | tf_op jit(solution)/shard_map/ppermute | solution.py:30
  69.0 34.0 %collective-permute-start.7 = (f32[4,4,64,1]{3,1,0,2:T(4,128)}, f32[4,4,64,1]{3,1,0,2:T(4,128)}, u32[]{:S(2)}, u32[]{:S(2)}) collective-permute-start(f32[4,4,64,1]{3,1,0,2:T(4,128)} %get-tuple-element.34), channel_id=1, source_target_pairs={{0,8},{8,16},{16,24},{24,0},{1,9},{9,17},{17,25},{25,1},{2,10},{10... | collective-permute-start | bytes 12296 | tf_op jit(solution)/shard_map/ppermute | solution.py:27
  69.4 33.6 %collective-permute-start.6 = (f32[4,4,64,1]{3,1,0,2:T(4,128)}, f32[4,4,64,1]{3,1,0,2:T(4,128)}, u32[]{:S(2)}, u32[]{:S(2)}) collective-permute-start(f32[4,4,64,1]{3,1,0,2:T(4,128)} %get-tuple-element.35), channel_id=1, source_target_pairs={{8,0},{16,8},{24,16},{0,24},{9,1},{17,9},{25,17},{1,25},{10,2},{18... | collective-permute-start | bytes 12296 | tf_op jit(solution)/shard_map/ppermute | solution.py:30
where the time goes:
time: 110 us; the launch traced here: 109 us
  blocking collectives  37.9 us (34%)
  local copies, waits for them, and re-layouts  25.1 us (23%)
  starting transfers between devices  18.5 us (17%)
  other arithmetic  14.9 us (14%)
  waiting for transfers between devices  12.3 us (11%)
    all_gather x2, blocking collectives, per_device(): whole_row = lax.all_gather(fold_flux, 'lon', axis=2, tiled=True)  37.9 us
    ppermute x4, waiting for transfers between devices, with_halo(): lax.ppermute(lax.slice_in_dim(block, 0, width, axis=dim), axis, backward)  12.2 us
    add x2, other arithmetic, per_device(): total = masked + transport  8.75 us
    ppermute x4, starting transfers between devices, with_halo(): lax.ppermute(lax.slice_in_dim(block, 0, width, axis=dim), axis, backward)  8 us
    gather x4, local copies, waits for them, and re-layouts, per_device(): picked = jnp.take(whole_row, partner, axis=2)  7.4 us
    ppermute x4, starting transfers between devices, with_halo(): lax.ppermute(lax.slice_in_dim(block, block.shape[dim] - width, None, axis...  7.11 us
    slice x2, local copies, waits for them, and re-layouts, per_device(): masked[:, :, :-1, :]  3.65 us
    all_gather x2, local copies, waits for them, and re-layouts, per_device(): whole_row = lax.all_gather(fold_flux, 'lon', axis=2, tiled=True)  3.41 us
  transfers between devices with their start and end apart: 10, of which 1 were waited for; matrix products, arithmetic and copies ran while one was open for 22% of the time, Pallas kernels for 0%

commit v1 on v0

--- a/solution.py
+++ b/solution.py
@@ -4,6 +4,24 @@
 from jax.sharding import PartitionSpec as P
 
 STEPS = 2
+
+
+def joined_along(blocks, dim):
+    lengths = list(blocks.shape[1:])
+    lengths[dim] *= blocks.shape[0]
+    return jnp.moveaxis(blocks, 0, dim).reshape(lengths)
+
+
+def doubled(x, axis):
+    size = lax.axis_size(axis)
+    tiles = x[None]
+    for level in range(size.bit_length() - 1):
+        bit = 1 << level
+        theirs = lax.ppermute(tiles, axis, [(i, i ^ bit) for i in range(size)])
+        both = jnp.stack([tiles, theirs])
+        upper = lax.axis_index(axis) >> level & 1
+        tiles = jnp.where(upper == 0, both, both[::-1]).reshape(-1, *x.shape)
+    return tiles
 
 
 def shifted(shard, axis, by):
@@ -63,7 +81,7 @@
             + 0.5 * south_speed * (masked - south_adj)
         )
         fold_flux = fold_weight * masked[:, :, -1, :]
-        whole_row = lax.all_gather(fold_flux, "lon", axis=2, tiled=True)
+        whole_row = joined_along(doubled(fold_flux, "lon"), 2)
         picked = jnp.take(whole_row, partner, axis=2)
         folded = 0.5 * fold_signs * picked
         total = masked + transport

time: 110 us -> 102 us (0.927)
  blocking collectives: 37.9 us -> 0 us
  waiting for transfers between devices: 12.3 us -> 43.5 us
  local copies, waits for them, and re-layouts: 25.1 us -> 19.7 us
  starting transfers between devices: 18.5 us -> 23.1 us
    all_gather x2 -> x0, blocking collectives: 37.9 us -> none  [per_device(): whole_row = lax.all_gather(fold_flux, 'lon', axis=2, tiled=True)]
    ppermute x4, waiting for transfers between devices: 0.01 us -> 21.1 us  [with_halo(): lax.ppermute(lax.slice_in_dim(block, block.shape[dim] - width, None, axis...]
    ppermute x4, waiting for transfers between devices: 12.2 us -> 22.4 us  [with_halo(): lax.ppermute(lax.slice_in_dim(block, 0, width, axis=dim), axis, backward)]
    ppermute x0 -> x4, starting transfers between devices: none -> 4.29 us  [doubled(): theirs = lax.ppermute(tiles, axis, [(i, i ^ bit) for i in range(size)])]
    all_gather x2 -> x0, local copies, waits for them, and re-layouts: 3.41 us -> none  [per_device(): whole_row = lax.all_gather(fold_flux, 'lon', axis=2, tiled=True)]
    reshape x0 -> x2, local copies, waits for them, and re-layouts: none -> 2.63 us  [joined_along(): return jnp.moveaxis(blocks, 0, dim).reshape(lengths)]
    add x2, other arithmetic: 8.75 us -> 7.06 us  [per_device(): total = masked + transport]
    gather x4, local copies, waits for them, and re-layouts: 7.4 us -> 5.78 us  [per_device(): picked = jnp.take(whole_row, partner, axis=2)]
  transfers between devices with their start and end apart: 10 -> 14, of which waited for: 1 -> 4; matrix products, arithmetic and copies ran while one was open for 22% -> 21% of each run, Pallas kernels for 0% -> 0%
where the time goes in v1:
time: 102 us; the launch traced here: 101 us
  waiting for transfers between devices  43.5 us (43%)
  starting transfers between devices  23.1 us (23%)
  local copies, waits for them, and re-layouts  19.7 us (19%)
  other arithmetic  14.4 us (14%)
    ppermute x4, waiting for transfers between devices, with_halo(): lax.ppermute(lax.slice_in_dim(block, 0, width, axis=dim), axis, backward)  22.4 us
    ppermute x4, waiting for transfers between devices, with_halo(): lax.ppermute(lax.slice_in_dim(block, block.shape[dim] - width, None, axis...  21.1 us
    ppermute x4, starting transfers between devices, with_halo(): lax.ppermute(lax.slice_in_dim(block, block.shape[dim] - width, None, axis...  7.91 us
    ppermute x4, starting transfers between devices, with_halo(): lax.ppermute(lax.slice_in_dim(block, 0, width, axis=dim), axis, backward)  7.4 us
    add x2, other arithmetic, per_device(): total = masked + transport  7.06 us
    gather x4, local copies, waits for them, and re-layouts, per_device(): picked = jnp.take(whole_row, partner, axis=2)  5.78 us
    ppermute x4, starting transfers between devices, doubled(): theirs = lax.ppermute(tiles, axis, [(i, i ^ bit) for i in range(size)])  4.29 us
    reshape x2, local copies, waits for them, and re-layouts, joined_along(): return jnp.moveaxis(blocks, 0, dim).reshape(lengths)  2.63 us
  transfers between devices with their start and end apart: 14, of which 4 were waited for; matrix products, arithmetic and copies ran while one was open for 21% of the time, Pallas kernels for 0%

profile of v1, /device:TPU:10, one launch (start us, length us, event | category | flops | bytes accessed | tf_op | source)
XLA Modules:
  0.0 101.3 jit_solution(9739158607010157350)
XLA Ops:
  0.0 0.8 broadcast_add_fusion
  0.8 2.1 %collective-permute-start.4 = (f32[4,1,256]{2,1,0:T(1,128)S(1)}, f32[4,1,256]{2,1,0:T(1,128)S(1)}, u32[]{:S(2)}, u32[]{:S(2)}) collective-permute-start(f32[4,1,256]{2,1,0:T(1,128)S(1)} %get-tuple-element.47), channel_id=1, source_target_pairs={{0,1},{1,2},{2,3},{3,4},{4,5},{5,6},{6,7},{8,9},{9,10},{10,11},{11... | collective-permute-start | bytes 12296 | tf_op jit(solution)/shard_map/ppermute | solution.py:35
  2.9 1.7 %slice.119 = f32[4,64,1]{2,1,0:T(8,128)} slice(f32[4,64,256]{2,1,0:T(8,128)} %param.13), slice={[0:4], [0:64], [255:256]} | slice | bytes 2048 | tf_op jit(solution)/shard_map/slice | solution.py:59
  4.5 1.5 %collective-permute-start.1 = (f32[4,64,1]{2,1,0:T(8,128)}, f32[4,64,1]{2,1,0:T(8,128)S(1)}, u32[]{:S(2)}, u32[]{:S(2)}) collective-permute-start(f32[4,64,1]{2,1,0:T(8,128)} %slice.119), channel_id=1, source_target_pairs={{0,8},{8,16},{16,24},{24,0},{1,9},{9,17},{17,25},{25,1},{2,10},{10... | collective-permute-start | bytes 3080 | tf_op jit(solution)/shard_map/ppermute | solution.py:29
  6.0 1.0 convert_element_type.6
  7.0 0.2 copy.101
  7.2 2.0 %copy_multiply_fusion = f32[4,4,64,256]{3,1,0,2:T(4,128)S(1)} fusion(f32[4,4,64,256]{3,2,1,0:T(8,128)} %param.12, f32[4,64,256]{2,0,1:T(4,128)S(1)} %copy.101), kind=kLoop, calls=%fused_computation.26 | loop fusion | flops 262144 | bytes 2359296 | tf_op jit(solution)/shard_map/mul | solution.py:66
  9.2 0.6 bitcast_multiply_fusion.4
  9.8 0.5 collective-permute-start.6
  10.3 0.6 fusion.28
  11.0 3.0 %collective-permute-start.5 = (f32[4,4,1,256]{3,1,0,2:T(4,128)}, f32[4,4,1,256]{3,1,0,2:T(4,128)}, u32[]{:S(2)}, u32[]{:S(2)}) collective-permute-start(f32[4,4,1,256]{3,1,0,2:T(4,128)} %get-tuple-element.38), channel_id=1, source_target_pairs={{0,1},{1,2},{2,3},{3,4},{4,5},{5,6},{6,7},{8,9},{9,10},{10,11},{11... | collective-permute-start | bytes 49160 | tf_op jit(solution)/shard_map/ppermute | solution.py:45
  14.0 2.5 %collective-permute-start.3 = (f32[4,4,1,256]{3,1,0,2:T(4,128)}, f32[4,4,1,256]{3,1,0,2:T(4,128)}, u32[]{:S(2)}, u32[]{:S(2)}) collective-permute-start(f32[4,4,1,256]{3,1,0,2:T(4,128)} %get-tuple-element.39), channel_id=1, source_target_pairs={{1,0},{2,1},{3,2},{4,3},{5,4},{6,5},{7,6},{9,8},{10,9},{11,10},{12... | collective-permute-start | bytes 49160 | tf_op jit(solution)/shard_map/ppermute | solution.py:48
  16.5 0.5 compare_and_fusion
  17.2 0.6 bitcast_multiply_fusion.5
  17.8 1.3 %fusion.30 = (f32[4,4,64,1]{3,1,0,2:T(4,128)}, f32[4,4,64,1]{3,1,0,2:T(4,128)}) fusion(f32[4,4,64,256]{3,1,0,2:T(4,128)S(1)} %copy_multiply_fusion), kind=kLoop, calls=%fused_computation.68 | loop fusion | bytes 16384 | tf_op jit(solution)/shard_map/slice | solution.py:46
  19.1 1.9 %fusion.29 = (f32[4,4,63,256]{3,1,0,2:T(4,128)}, f32[4,4,63,256]{3,1,0,2:T(4,128)}) fusion(f32[4,4,64,256]{3,1,0,2:T(4,128)S(1)} %copy_multiply_fusion), kind=kLoop, calls=%fused_computation.67 | loop fusion | bytes 4128768 | tf_op jit(solution)/shard_map/slice | solution.py:76
  21.0 1.7 %fusion.31 = (f32[4,4,64,255]{3,1,0,2:T(4,128)S(1)}, f32[4,4,64,255]{3,1,0,2:T(4,128)}) fusion(f32[4,4,64,256]{3,1,0,2:T(4,128)S(1)} %copy_multiply_fusion), kind=kLoop, calls=%fused_computation.69 | loop fusion | bytes 4177920 | tf_op jit(solution)/shard_map/slice | solution.py:74
  22.7 0.0 copy-start.1
  22.7 0.2 copy.103
  22.9 0.2 copy.105
  23.1 0.0 collective-permute-done.1
  23.1 1.5 %collective-permute-start.2 = (f32[4,4,64,1]{3,1,0,2:T(4,128)}, f32[4,4,64,1]{3,1,0,2:T(4,128)S(1)}, u32[]{:S(2)}, u32[]{:S(2)}) collective-permute-start(f32[4,4,64,1]{3,1,0,2:T(4,128)} %get-tuple-element.42), channel_id=1, source_target_pairs={{0,8},{8,16},{16,24},{24,0},{1,9},{9,17},{17,25},{25,1},{2,10},{10... | collective-permute-start | bytes 12296 | tf_op jit(solution)/shard_map/ppermute | solution.py:45
  24.6 0.1 maximum_multiply_fusion
  24.7 0.2 copy.104
  24.9 0.0 collective-permute-done.4
  24.9 0.6 collective-permute-start
  25.6 0.2 copy.106
  25.8 0.0 collective-permute-done.6
  25.8 0.8 pad_maximum_fusion.2
  26.6 1.6 %collective-permute-start.7 = (f32[2,4,4,256]{3,2,1,0:T(4,128)S(1)}, f32[2,4,4,256]{3,2,1,0:T(4,128)S(1)}, u32[]{:S(2)}, u32[]{:S(2)}) collective-permute-start(f32[2,4,4,256]{3,2,1,0:T(4,128)S(1)} %get-tuple-element.51), channel_id=1, source_target_pairs={{0,16},{8,24},{16,0},{24,8},{1,17},{9,25},{17,1},{25,9},{2,18},{10... | collective-permute-start | bytes 98312 | tf_op jit(solution)/shard_map/ppermute | solution.py:20
  28.2 10.0 %collective-permute-done.2 = f32[4,4,64,1]{3,1,0,2:T(4,128)S(1)} collective-permute-done((f32[4,4,64,1]{3,1,0,2:T(4,128)}, f32[4,4,64,1]{3,1,0,2:T(4,128)S(1)}, u32[]{:S(2)}, u32[]{:S(2)}) %collective-permute-start.2) | collective-permute-done | bytes 4128 | tf_op jit(solution)/shard_map/ppermute | solution.py:45
  38.1 11.2 %collective-permute-done = f32[4,4,64,1]{3,1,0,2:T(4,128)S(1)} collective-permute-done((f32[4,4,64,1]{3,1,0,2:T(4,128)}, f32[4,4,64,1]{3,1,0,2:T(4,128)S(1)}, u32[]{:S(2)}, u32[]{:S(2)}) %collective-permute-start) | collective-permute-done | bytes 4128 | tf_op jit(solution)/shard_map/ppermute | solution.py:48
  49.3 0.0 collective-permute-done.5
  49.3 0.0 collective-permute-done.3
  49.3 4.3 %fusion.4 = f32[4,4,64,256]{3,1,0,2:T(4,128)S(1)} fusion(f32[4,4,64,1]{3,1,0,2:T(4,128)S(1)} %collective-permute-done, f32[4,4,64,255]{3,1,0,2:T(4,128)S(1)} %copy-done.1, f32[4,4,64,255]{3,1,0,2:T(4,128)S(1)} %get-tuple-element.44, f32[4,4,64,1]{3,1,0,2:T(4,128)S(1)} %collective-permute-done.2, f32[4,4,1,256]{3,1,0,2:T(4,128)} %collective-permute-done.3, ...), kind=kLoop, calls=%fused_computation.7 | loop fusion | flops 4456448 | bytes 7602176 | tf_op jit(solution)/shard_map/add | solution.py:87
  53.7 0.0 copy-start.13
  53.7 0.0 collective-permute-done.7
  53.8 1.8 %copy.114 = f32[4,4,4,256]{1,0,3,2:T(4,128)} copy(f32[4,4,4,256]{3,1,0,2:T(4,128)S(1)} %bitcast.56) | data formatting | bytes 131072 | tf_op jit(solution)/shard_map/reshape | solution.py:12
  55.6 2.6 %gather_fusion = f32[256,4,4]{2,1,0:T(4,128)S(1)} fusion(f32[4,4,1024]{1,0,2:T(4,128)} %bitcast.52, s32[1024]{0:T(1024)S(1)} %pad_clamp_fusion), kind=kCustom, calls=%fused_computation.clone | custom fusion | bytes 33792 | tf_op jit(solution)/shard_map/jit(_take)/gather | solution.py:85
  58.2 0.2 copy.109
  58.4 0.1 fusion.21
  58.5 0.3 multiply_multiply_fusion
  58.8 0.3 fusion.26
  59.2 0.5 fusion.25
  59.7 0.7 fusion.27
  60.4 0.6 collective-permute-start.12
  61.0 1.9 %collective-permute-start.11 = (f32[4,4,1,256]{3,1,0,2:T(4,128)S(1)}, f32[4,4,1,256]{3,1,0,2:T(4,128)S(1)}, u32[]{:S(2)}, u32[]{:S(2)}) collective-permute-start(f32[4,4,1,256]{3,1,0,2:T(4,128)S(1)} %get-tuple-element.30), channel_id=1, source_target_pairs={{0,1},{1,2},{2,3},{3,4},{4,5},{5,6},{6,7},{8,9},{9,10},{10,11},{11... | collective-permute-start | bytes 49160 | tf_op jit(solution)/shard_map/ppermute | solution.py:45
  63.0 3.6 %collective-permute-start.10 = (f32[4,4,1,256]{3,1,0,2:T(4,128)S(1)}, f32[4,4,1,256]{3,1,0,2:T(4,128)S(1)}, u32[]{:S(2)}, u32[]{:S(2)}) collective-permute-start(f32[4,4,1,256]{3,1,0,2:T(4,128)S(1)} %get-tuple-element.31), channel_id=1, source_target_pairs={{1,0},{2,1},{3,2},{4,3},{5,4},{6,5},{7,6},{9,8},{10,9},{11,10},{12... | collective-permute-start | bytes 49160 | tf_op jit(solution)/shard_map/ppermute | solution.py:48
  66.6 1.5 %collective-permute-start.9 = (f32[4,4,64,1]{3,1,0,2:T(4,128)S(1)}, f32[4,4,64,1]{3,1,0,2:T(4,128)S(1)}, u32[]{:S(2)}, u32[]{:S(2)}) collective-permute-start(f32[4,4,64,1]{3,1,0,2:T(4,128)S(1)} %get-tuple-element.34), channel_id=1, source_target_pairs={{0,8},{8,16},{16,24},{24,0},{1,9},{9,17},{17,25},{25,1},{2,10},{10... | collective-permute-start | bytes 12296 | tf_op jit(solution)/shard_map/ppermute | solution.py:45
  68.1 0.6 collective-permute-start.8
  68.7 0.0 collective-permute-done.12
  68.7 1.6 %collective-permute-start.13 = (f32[2,4,4,256]{3,2,1,0:T(4,128)S(1)}, f32[2,4,4,256]{3,2,1,0:T(4,128)S(1)}, u32[]{:S(2)}, u32[]{:S(2)}) collective-permute-start(f32[2,4,4,256]{3,2,1,0:T(4,128)S(1)} %get-tuple-element.49), channel_id=1, source_target_pairs={{0,16},{8,24},{16,0},{24,8},{1,17},{9,25},{17,1},{25,9},{2,18},{10... | collective-permute-start | bytes 98312 | tf_op jit(solution)/shard_map/ppermute | solution.py:20
  70.3 11.1 %collective-permute-done.9 = f32[4,4,64,1]{3,1,0,2:T(4,128)S(1)} collective-permute-done((f32[4,4,64,1]{3,1,0,2:T(4,128)S(1)}, f32[4,4,64,1]{3,1,0,2:T(4,128)S(1)}, u32[]{:S(2)}, u32[]{:S(2)}) %collective-permute-start.9) | collective-permute-done | bytes 4128 | tf_op jit(solution)/shard_map/ppermute | solution.py:45
  81.5 11.2 %collective-permute-done.8 = f32[4,4,64,1]{3,1,0,2:T(4,128)S(1)} collective-permute-done((f32[4,4,64,1]{3,1,0,2:T(4,128)S(1)}, f32[4,4,64,1]{3,1,0,2:T(4,128)S(1)}, u32[]{:S(2)}, u32[]{:S(2)}) %collective-permute-start.8) | collective-permute-done | bytes 4128 | tf_op jit(solution)/shard_map/ppermute | solution.py:48
  92.6 0.0 collective-permute-done.11
  92.6 0.0 collective-permute-done.10
  92.7 2.7 %fusion.12 = f32[4,4,64,256]{3,1,0,2:T(4,128)S(1)} fusion(f32[4,4,64,1]{3,1,0,2:T(4,128)S(1)} %collective-permute-done.8, f32[4,4,64,255]{3,1,0,2:T(4,128)S(1)} %get-tuple-element.37, f32[4,4,64,255]{3,1,0,2:T(4,128)S(1)} %get-tuple-element.36, f32[4,4,64,1]{3,1,0,2:T(4,128)S(1)} %collective-permute-done.9, f32[4,4,1,256]{3,1,0,2:T(4,128)S(1)} %collective-permute-done.10, ...), kind=kLoop, calls=%fused_computation.19 | loop fusion | flops 4718592 | bytes 7602176 | tf_op jit(solution)/shard_map/add | solution.py:87
  95.4 0.0 collective-permute-done.13
  95.5 0.9 copy.115
  96.3 1.8 %gather_fusion.1 = f32[256,4,4]{2,1,0:T(4,128)} fusion(f32[4,4,1024]{1,0,2:T(4,128)S(1)} %bitcast.51, s32[1024]{0:T(1024)S(1)} %pad_clamp_fusion), kind=kCustom, calls=%fused_computation.1.clone | custom fusion | bytes 33792 | tf_op jit(solution)/shard_map/jit(_take)/gather | solution.py:85
  98.1 1.2 %copy.112 = f32[256,4,4]{0,2,1:T(4,128)S(1)} copy(f32[256,4,4]{2,1,0:T(4,128)} %gather_fusion.1) | data formatting | bytes 32768 | tf_op jit(solution)/shard_map/jit(_take)/gather | solution.py:85
  99.3 0.1 fusion.20
  99.4 0.3 broadcast_multiply_fusion
  99.7 1.6 %copy.113 = f32[4,4,64,256]{3,2,1,0:T(8,128)} copy(f32[4,4,64,256]{3,1,0,2:T(4,128)S(1)} %broadcast_multiply_fusion) | data formatting | bytes 2097152 | tf_op jit(solution)/shard_map/mul | solution.py:89
  (46 shorter events, 0.3 us)
Async XLA Ops:
  0.0 17.1 %copy-start.10 = (f32[4,64,256]{2,1,0:T(8,128)S(1)}, f32[4,64,256]{2,1,0:T(8,128)}, u32[]{:S(2)}) copy-start(f32[4,64,256]{2,1,0:T(8,128)} %param.13) | copy-start | bytes 786436
  0.0 16.5 %copy-start.15 = (s32[256]{0:T(256)S(1)}, s32[256]{0:T(256)}, u32[]{:S(2)}) copy-start(s32[256]{0:T(256)} %param.16) | copy-start | bytes 3076
  0.8 16.3 %copy-start.11 = (f32[4,64,256]{2,1,0:T(8,128)S(1)}, f32[4,64,256]{2,1,0:T(8,128)}, u32[]{:S(2)}) copy-start(f32[4,64,256]{2,1,0:T(8,128)} %param.14) | copy-start | bytes 786436
  0.8 24.1 %collective-permute-start.4 = (f32[4,1,256]{2,1,0:T(1,128)S(1)}, f32[4,1,256]{2,1,0:T(1,128)S(1)}, u32[]{:S(2)}, u32[]{:S(2)}) collective-permute-start(f32[4,1,256]{2,1,0:T(1,128)S(1)} %get-tuple-element.47), channel_id=1, source_target_pairs={{0,1},{1,2},{2,3},{3,4},{4,5},{5,6},{6,7},{8,9},{9,10},{10,11},{11... | collective-permute-start | bytes 12296 | tf_op jit(solution)/shard_map/ppermute | solution.py:35
  4.5 18.5 %collective-permute-start.1 = (f32[4,64,1]{2,1,0:T(8,128)}, f32[4,64,1]{2,1,0:T(8,128)S(1)}, u32[]{:S(2)}, u32[]{:S(2)}) collective-permute-start(f32[4,64,1]{2,1,0:T(8,128)} %slice.119), channel_id=1, source_target_pairs={{0,8},{8,16},{16,24},{24,0},{1,9},{9,17},{17,25},{25,1},{2,10},{10... | collective-permute-start | bytes 3080 | tf_op jit(solution)/shard_map/ppermute | solution.py:29
  9.8 16.0 %collective-permute-start.6 = (f32[1,4,4,256]{3,2,1,0:T(4,128)}, f32[1,4,4,256]{3,2,1,0:T(4,128)}, u32[]{:S(2)}, u32[]{:S(2)}) collective-permute-start(f32[1,4,4,256]{3,2,1,0:T(4,128)} %bitcast_multiply_fusion.4), channel_id=1, source_target_pairs={{0,8},{8,0},{16,24},{24,16},{1,9},{9,1},{17,25},{25,17},{2,10},{10... | collective-permute-start | bytes 49160 | tf_op jit(solution)/shard_map/ppermute | solution.py:20
  11.0 38.4 %collective-permute-start.5 = (f32[4,4,1,256]{3,1,0,2:T(4,128)}, f32[4,4,1,256]{3,1,0,2:T(4,128)}, u32[]{:S(2)}, u32[]{:S(2)}) collective-permute-start(f32[4,4,1,256]{3,1,0,2:T(4,128)} %get-tuple-element.38), channel_id=1, source_target_pairs={{0,1},{1,2},{2,3},{3,4},{4,5},{5,6},{6,7},{8,9},{9,10},{10,11},{11... | collective-permute-start | bytes 49160 | tf_op jit(solution)/shard_map/ppermute | solution.py:45
  14.0 35.3 %collective-permute-start.3 = (f32[4,4,1,256]{3,1,0,2:T(4,128)}, f32[4,4,1,256]{3,1,0,2:T(4,128)}, u32[]{:S(2)}, u32[]{:S(2)}) collective-permute-start(f32[4,4,1,256]{3,1,0,2:T(4,128)} %get-tuple-element.39), channel_id=1, source_target_pairs={{1,0},{2,1},{3,2},{4,3},{5,4},{6,5},{7,6},{9,8},{10,9},{11,10},{12... | collective-permute-start | bytes 49160 | tf_op jit(solution)/shard_map/ppermute | solution.py:48
  22.7 26.7 %copy-start = (f32[4,4,64,256]{3,2,1,0:T(8,128)S(1)}, f32[4,4,64,256]{3,2,1,0:T(8,128)}, u32[]{:S(2)}) copy-start(f32[4,4,64,256]{3,2,1,0:T(8,128)} %param.12) | copy-start | bytes 3145732
  22.7 3.1 %copy-start.12 = (f32[1,1,4,4,256]{4,3,2,1,0:T(4,128)S(1)}, f32[1,1,4,4,256]{4,3,2,1,0:T(4,128)}, u32[]{:S(2)}) copy-start(f32[1,1,4,4,256]{4,3,2,1,0:T(4,128)} %bitcast_multiply_fusion.5) | copy-start | bytes 49156
  22.7 26.7 %copy-start.1 = (f32[4,4,64,255]{3,1,0,2:T(4,128)S(1)}, f32[4,4,64,255]{3,1,0,2:T(4,128)}, u32[]{:S(2)}) copy-start(f32[4,4,64,255]{3,1,0,2:T(4,128)} %get-tuple-element.45) | copy-start | bytes 3133444
  22.9 30.8 %copy-start.2 = (f32[4,64,256]{2,0,1:T(4,128)}, f32[4,64,256]{2,0,1:T(4,128)S(1)}, u32[]{:S(2)}) copy-start(f32[4,64,256]{2,0,1:T(4,128)S(1)} %copy.103) | copy-start | bytes 786436
  23.1 30.6 %copy-start.4 = (f32[4,64,256]{2,0,1:T(4,128)}, f32[4,64,256]{2,0,1:T(4,128)S(1)}, u32[]{:S(2)}) copy-start(f32[4,64,256]{2,0,1:T(4,128)S(1)} %copy.105) | copy-start | bytes 786436
  23.1 15.1 %collective-permute-start.2 = (f32[4,4,64,1]{3,1,0,2:T(4,128)}, f32[4,4,64,1]{3,1,0,2:T(4,128)S(1)}, u32[]{:S(2)}, u32[]{:S(2)}) collective-permute-start(f32[4,4,64,1]{3,1,0,2:T(4,128)} %get-tuple-element.42), channel_id=1, source_target_pairs={{0,8},{8,16},{16,24},{24,0},{1,9},{9,17},{17,25},{25,1},{2,10},{10... | collective-permute-start | bytes 12296 | tf_op jit(solution)/shard_map/ppermute | solution.py:45
  24.9 28.8 %copy-start.6 = (f32[4,64,256]{2,0,1:T(4,128)}, f32[4,64,256]{2,0,1:T(4,128)S(1)}, u32[]{:S(2)}) copy-start(f32[4,64,256]{2,0,1:T(4,128)S(1)} %copy.104) | copy-start | bytes 786436
  24.9 24.4 %collective-permute-start = (f32[4,4,64,1]{3,1,0,2:T(4,128)}, f32[4,4,64,1]{3,1,0,2:T(4,128)S(1)}, u32[]{:S(2)}, u32[]{:S(2)}) collective-permute-start(f32[4,4,64,1]{3,1,0,2:T(4,128)} %get-tuple-element.43), channel_id=1, source_target_pairs={{8,0},{16,8},{24,16},{0,24},{9,1},{17,9},{25,17},{1,25},{10,2},{18... | collective-permute-start | bytes 12296 | tf_op jit(solution)/shard_map/ppermute | solution.py:48
  25.8 28.0 %copy-start.8 = (f32[4,64,256]{2,0,1:T(4,128)}, f32[4,64,256]{2,0,1:T(4,128)S(1)}, u32[]{:S(2)}) copy-start(f32[4,64,256]{2,0,1:T(4,128)S(1)} %copy.106) | copy-start | bytes 786436
  26.6 27.2 %collective-permute-start.7 = (f32[2,4,4,256]{3,2,1,0:T(4,128)S(1)}, f32[2,4,4,256]{3,2,1,0:T(4,128)S(1)}, u32[]{:S(2)}, u32[]{:S(2)}) collective-permute-start(f32[2,4,4,256]{3,2,1,0:T(4,128)S(1)} %get-tuple-element.51), channel_id=1, source_target_pairs={{0,16},{8,24},{16,0},{24,8},{1,17},{9,25},{17,1},{25,9},{2,18},{10... | collective-permute-start | bytes 98312 | tf_op jit(solution)/shard_map/ppermute | solution.py:20
  53.7 4.7 %copy-start.13 = (f32[4]{0:T(128)S(1)}, f32[4]{0:T(128)}, u32[]{:S(2)}) copy-start(f32[4]{0:T(128)} %constant.80) | copy-start | bytes 52
  53.7 4.6 %copy-start.14 = (pred[256]{0:T(512)(128)(4,1)S(1)}, pred[256]{0:T(512)(128)(4,1)}, u32[]{:S(2)}) copy-start(pred[256]{0:T(512)(128)(4,1)} %compare_and_fusion) | copy-start | bytes 772
  59.7 33.0 %copy-start.3 = (f32[4,64,256]{2,0,1:T(4,128)S(1)}, f32[4,64,256]{2,0,1:T(4,128)}, u32[]{:S(2)}) copy-start(f32[4,64,256]{2,0,1:T(4,128)} %copy-done.2) | copy-start | bytes 786436
  59.7 33.0 %copy-start.5 = (f32[4,64,256]{2,0,1:T(4,128)S(1)}, f32[4,64,256]{2,0,1:T(4,128)}, u32[]{:S(2)}) copy-start(f32[4,64,256]{2,0,1:T(4,128)} %copy-done.4) | copy-start | bytes 786436
  59.7 33.0 %copy-start.7 = (f32[4,64,256]{2,0,1:T(4,128)S(1)}, f32[4,64,256]{2,0,1:T(4,128)}, u32[]{:S(2)}) copy-start(f32[4,64,256]{2,0,1:T(4,128)} %copy-done.6) | copy-start | bytes 786436
  59.7 33.0 %copy-start.9 = (f32[4,64,256]{2,0,1:T(4,128)S(1)}, f32[4,64,256]{2,0,1:T(4,128)}, u32[]{:S(2)}) copy-start(f32[4,64,256]{2,0,1:T(4,128)} %copy-done.8) | copy-start | bytes 786436
  60.4 8.2 %collective-permute-start.12 = (f32[1,4,4,256]{3,2,1,0:T(4,128)S(1)}, f32[1,4,4,256]{3,2,1,0:T(4,128)S(1)}, u32[]{:S(2)}, u32[]{:S(2)}) collective-permute-start(f32[1,4,4,256]{3,2,1,0:T(4,128)S(1)} %bitcast_multiply_fusion.1), channel_id=1, source_target_pairs={{0,8},{8,0},{16,24},{24,16},{1,9},{9,1},{17,25},{25,17},{2,10},{10... | collective-permute-start | bytes 49160 | tf_op jit(solution)/shard_map/ppermute | solution.py:20
  61.0 31.6 %collective-permute-start.11 = (f32[4,4,1,256]{3,1,0,2:T(4,128)S(1)}, f32[4,4,1,256]{3,1,0,2:T(4,128)S(1)}, u32[]{:S(2)}, u32[]{:S(2)}) collective-permute-start(f32[4,4,1,256]{3,1,0,2:T(4,128)S(1)} %get-tuple-element.30), channel_id=1, source_target_pairs={{0,1},{1,2},{2,3},{3,4},{4,5},{5,6},{6,7},{8,9},{9,10},{10,11},{11... | collective-permute-start | bytes 49160 | tf_op jit(solution)/shard_map/ppermute | solution.py:45
  63.0 29.7 %collective-permute-start.10 = (f32[4,4,1,256]{3,1,0,2:T(4,128)S(1)}, f32[4,4,1,256]{3,1,0,2:T(4,128)S(1)}, u32[]{:S(2)}, u32[]{:S(2)}) collective-permute-start(f32[4,4,1,256]{3,1,0,2:T(4,128)S(1)} %get-tuple-element.31), channel_id=1, source_target_pairs={{1,0},{2,1},{3,2},{4,3},{5,4},{6,5},{7,6},{9,8},{10,9},{11,10},{12... | collective-permute-start | bytes 49160 | tf_op jit(solution)/shard_map/ppermute | solution.py:48
  66.6 14.8 %collective-permute-start.9 = (f32[4,4,64,1]{3,1,0,2:T(4,128)S(1)}, f32[4,4,64,1]{3,1,0,2:T(4,128)S(1)}, u32[]{:S(2)}, u32[]{:S(2)}) collective-permute-start(f32[4,4,64,1]{3,1,0,2:T(4,128)S(1)} %get-tuple-element.34), channel_id=1, source_target_pairs={{0,8},{8,16},{16,24},{24,0},{1,9},{9,17},{17,25},{25,1},{2,10},{10... | collective-permute-start | bytes 12296 | tf_op jit(solution)/shard_map/ppermute | solution.py:45
  68.1 24.5 %collective-permute-start.8 = (f32[4,4,64,1]{3,1,0,2:T(4,128)S(1)}, f32[4,4,64,1]{3,1,0,2:T(4,128)S(1)}, u32[]{:S(2)}, u32[]{:S(2)}) collective-permute-start(f32[4,4,64,1]{3,1,0,2:T(4,128)S(1)} %get-tuple-element.35), channel_id=1, source_target_pairs={{8,0},{16,8},{24,16},{0,24},{9,1},{17,9},{25,17},{1,25},{10,2},{18... | collective-permute-start | bytes 12296 | tf_op jit(solution)/shard_map/ppermute | solution.py:48
  68.7 26.7 %collective-permute-start.13 = (f32[2,4,4,256]{3,2,1,0:T(4,128)S(1)}, f32[2,4,4,256]{3,2,1,0:T(4,128)S(1)}, u32[]{:S(2)}, u32[]{:S(2)}) collective-permute-start(f32[2,4,4,256]{3,2,1,0:T(4,128)S(1)} %get-tuple-element.49), channel_id=1, source_target_pairs={{0,16},{8,24},{16,0},{24,8},{1,17},{9,25},{17,1},{25,9},{2,18},{10... | collective-permute-start | bytes 98312 | tf_op jit(solution)/shard_map/ppermute | solution.py:20
